TPU v7x, 128 devices: a whole 4x4x4 slice. The times are simulated.
128 devices in a mesh: tm: 16 (over y, x), orb: 8 (over z, core).
Axes of the slice: x: 4, y: 4, z: 4, core: 2. Of those that a mesh axis runs over, the one named last changes fastest.
Arguments:
- forward: bfloat16 [2, 2, 512, 128, 128], P(None, None, 'tm'), may hold values from -2 to 2
- backward_slab: bfloat16 [2, 2, 512, 128, 128], P(None, None, 'tm', 'orb'), may hold values from -2 to 2
- slot_time: int32 [512], replicated, may hold values from 0 to 511, as said below
- pattern: int32 [128, 128], replicated, may hold values 0 or 1
- coupling: float32 [128, 128], replicated, may hold values from -1 to 1
- hamiltonian: float32 [128, 128], replicated, may hold values from -0.8 to 0.8
- lesser_now: float32 [2, 128, 128], replicated, may hold values from -1.5 to 1.5
Outputs:
- lesser_next: float32 [2, 128, 128], P(None, 'orb')
Inputs may be any that keep to these rules, and one draw needn't show every extreme that they name: slot_time is a permutation of the 512 history times. The 32 slots of each index d of tm hold exactly 32 // 16 times of the range [e * 32, (e + 1) * 32) for every index e of tm.
All inputs are finite; a program needn't handle non-finite values.
Results may differ from a plain program's by a relative error of at most 0.0054.
Values may be sent and summed in bfloat16 or wider, within the bound.
No kernel may reach another device: no remote copies, remote signals or barrier semaphores. Data moves between devices by JAX's collectives and lax.ppermute only.
A program may use at most 64 MiB of HBM per device.

v0:
```python
import jax
import jax.numpy as jnp
from jax import lax
from jax.experimental import pallas as pl
from jax.experimental.pallas import tpu as pltpu
from jax.sharding import PartitionSpec as P


N = 128
bf = jnp.bfloat16
f32 = jnp.float32
HISTORY_STEP = 0.02
UPDATE_STEP = 0.5
STEPS = N // 8
UNITS = [(kk, a) for kk in range(4) for a in range(2)]


def rows16(row):
    return jnp.broadcast_to(row, (16, N)).astype(bf)


def cat0(parts):
    return jnp.concatenate(parts, axis=0)


def cat1(parts):
    return jnp.concatenate(parts, axis=1)


def shift(orb, half):
    down = 2 * (orb & 1) + half
    return down, (down + (orb >> 1)) & 3


def matches(times, row, holder):
    early = jnp.int32(1 << 20)
    late = jnp.int32(-1)
    for slot in range(32):
        when = times[row + slot]
        mine = (when >> 5) == holder
        key = slot * 512 + when
        early = jnp.minimum(early, jnp.where(mine, key, 1 << 20))
        late = jnp.maximum(late, jnp.where(mine, key, -1))
    return early & 511, late & 511


def collide(times, f0, f1, brecv, coup, patt, out, vb, vv, ft, bt, dirt, sig, wts):
    masked = coup[...] * patt[...].astype(f32)
    inter = ((masked + masked.T) * 0.5).astype(bf)
    vv[...] = inter.astype(f32)

    def fmat(kk, a, c):
        return (f0, f1)[kk // 2][kk % 2, a, c]

    def bmat(kk, a, c):
        return cat0([brecv[o, 1 - a, c, kk] for o in range(8)])

    def direct(*accs):
        me = lax.axis_index("tm")
        for half in range(2):
            dy, dx = shift(lax.axis_index("orb"), half)
            holder = ((((me >> 2) - dy) & 3) << 2) + (((me & 3) - dx) & 3)
            for r, when in enumerate(matches(times, me << 5, holder)):
                edge = jnp.logical_or(when == 0, when == 511)
                weight = jnp.where(edge, jnp.float32(0.5), jnp.float32(1.0)) * jnp.float32(HISTORY_STEP)
                wts[2 * half + r] = weight
        zero = jnp.zeros((N, N), bf)
        wide = jnp.zeros((N, 2 * N), bf)
        for u, (kk, a) in enumerate(UNITS):
            fr = fmat(kk, a, 0).astype(f32)
            fi = fmat(kk, a, 1).astype(f32)
            tr = bmat(kk, a, 0).T.astype(f32)
            ti = bmat(kk, a, 1).T.astype(f32)
            ft[u, 0] = fr
            ft[u, 1] = fi
            bt[u, 0] = tr
            bt[u, 1] = ti
            bub = cat1([(fr * tr - fi * ti).astype(bf), (fr * ti + fi * tr).astype(bf)])
            stage = (u // 2) % 2
            pltpu.matmul_push_rhs(cat0([bub, wide]), stage, u % 2)
            pltpu.matmul_acc_lhs(accs[u], cat1([inter, zero]), load_staged_rhs=stage)
        both = cat0([cat1([inter, zero]), cat1([zero, inter])])
        for x in range(2):
            pltpu.matmul_push_rhs(both, 0, x)
        lefts = [pltpu.matmul_pop(accs[u]).astype(bf) for u in range(8)]
        for u in range(8):
            pltpu.matmul_acc_lhs(accs[u], lefts[u], load_staged_rhs=0 if u < 2 else None)
        for u in range(8):
            scr = pltpu.matmul_pop(accs[u])
            fr, fi = ft[u, 0], ft[u, 1]
            sr, si = scr[:, :N], scr[:, N:]
            dirt[u, :, :N] = fr * sr - fi * si
            dirt[u, :, N:] = fr * si + fi * sr

    pl.run_scoped(direct, *[pltpu.ACC(u % 2)((N, 2 * N), f32) for u in range(8)])

    def weights(u, m):
        half = []
        for x in range(2):
            fvr = rows16(ft[u, 0, pl.ds(m + x, 1), :])
            fvi = rows16(ft[u, 1, pl.ds(m + x, 1), :])
            v = [vv[16 * i:16 * i + 16].astype(bf) for i in range(8)]
            half.append(cat1([cat0([w * fvr for w in v]), cat0([w * fvi for w in v])]))
        return cat0(half)

    def lhs_rows(u, m, first):
        re, im = [], []
        for x in range(2):
            bvr = rows16(bt[u, 0, pl.ds(m + x, 1), :])
            bvi = rows16(bt[u, 1, pl.ds(m + x, 1), :])
            pr, pi = [], []
            for i in range(8):
                sl = slice(16 * i, 16 * i + 16)
                a = ft[u, 0, sl].astype(bf)
                b = ft[u, 1, sl].astype(bf)
                if first:
                    wide = jnp.broadcast_to(vv[sl, m + x:m + x + 1], (16, N))
                    vb[m + x, sl] = wide
                else:
                    wide = vb[m + x, sl]
                v = wide.astype(bf)
                pr.append((a * bvr - b * bvi) * v)
                pi.append((a * bvi + b * bvr) * v)
            re.append(cat0(pr))
            im.append(cat0(pi))
        return cat1(re), cat1(im)

    def exchange(*flat):
        def step(u, par, t, first=False, last=False):
            acc = flat[4 * par:4 * par + 4]
            for q in range(2):
                base = 8 * t + 4 * q
                lhs = [lhs_rows(u, base + 2 * x, first) for x in range(2)]
                for x in range(2):
                    pltpu.matmul_acc_lhs(acc[2 * x], lhs[x][0], load_staged_rhs=q)
                if not (last and q):
                    for x in range(2):
                        pltpu.matmul_push_rhs(weights(u, base + 4 + 2 * x), 1 - q, x)
                elif not (isinstance(u, int) and u == 7):
                    for x in range(2):
                        pltpu.matmul_push_rhs(weights(u + 1, 2 * x), 0, x)
                for x in range(2):
                    pltpu.matmul_acc_lhs(acc[2 * x + 1], lhs[x][1])

        def finish(u, par):
            acc = flat[4 * par:4 * par + 4]
            rp = pltpu.matmul_pop(acc[0]) + pltpu.matmul_pop(acc[2])
            rq = pltpu.matmul_pop(acc[1]) + pltpu.matmul_pop(acc[3])
            sig[u, :, :N] = (dirt[u, :, :N] - (rp[:, :N] - rq[:, N:])).astype(bf)
            sig[u, :, N:] = (dirt[u, :, N:] - (rp[:, N:] + rq[:, :N])).astype(bf)

        def unit(u, par):
            step(u, par, 0)
            finish(u - 1, 1 - par)

            def loop(t, inner):
                step(u, par, t)
                return inner

            lax.fori_loop(1, STEPS - 1, loop, 0, unroll=7)
            step(u, par, STEPS - 1, last=True)

        def pair(p, carry):
            unit(2 * p + 1, 1)
            unit(2 * p + 2, 0)
            return carry

        for x in range(2):
            pltpu.matmul_push_rhs(weights(0, 2 * x), 0, x)
        for t in range(STEPS):
            step(0, 0, t, first=True, last=t == STEPS - 1)
        lax.fori_loop(0, 3, pair, 0)
        unit(7, 1)
        finish(7, 1)

    pl.run_scoped(exchange, *[pltpu.ACC(x)((N, 2 * N), f32) for x in (0, 0, 1, 1, 0, 0, 1, 1)])

    def product(*accs):
        for u, (kk, a) in enumerate(UNITS):
            br = bmat(kk, a, 0)
            bi = bmat(kk, a, 1)
            if a:
                br, bi = -br, -bi
            pltpu.matmul_push_rhs(cat0([cat1([br, bi]), cat1([-bi, br])]), a, kk % 2)
            pltpu.matmul_acc_lhs(accs[kk], sig[u], load_staged_rhs=a)
        total = wts[0] * pltpu.matmul_pop(accs[0])
        for kk in range(1, 4):
            total += wts[kk] * pltpu.matmul_pop(accs[kk])
        re = total[:, :N]
        im = total[:, N:]
        back_re = -0.5 * (re + re.T)
        back_im = 0.5 * (im - im.T)
        for o in range(8):
            out[o, 0] = back_im[16 * o:16 * o + 16]
            out[o, 1] = back_re[16 * o:16 * o + 16]

    pl.run_scoped(product, *[pltpu.ACC(kk % 2)((N, 2 * N), f32) for kk in range(4)])


def pack(times, fwd, slab, bsend, f0, f1, here, placed, slices, seen, sems):
    me = lax.axis_index("tm")
    orb = lax.axis_index("orb")
    down = me >> 2
    right = me & 3
    rows_in = pltpu.make_async_copy(slab, here, sems.at[4])
    rows_in.start()
    copies = []
    for half, dst in enumerate((f0, f1)):
        dy, dx = shift(orb, half)
        row = ((((down + dy) & 3) << 2) + ((right + dx) & 3)) << 5
        for r, when in enumerate(matches(times, row, me)):
            spot = 2 * half + r
            copy = pltpu.make_async_copy(fwd.at[:, :, when & 31], slices.at[spot], sems.at[spot])
            copy.start()
            copies.append((copy, pltpu.make_async_copy(slices.at[spot], dst.at[r], sems.at[6 + spot])))
    for e in range(16):
        seen[e] = 0
    rows_in.wait()
    for slot in range(32):
        when = times[(me << 5) + slot]
        holder = when >> 5
        rank = seen[holder]
        seen[holder] = rank + 1
        dy = (down - (holder >> 2)) & 3
        dx = (right - (holder & 3)) & 3
        to = (((dx - dy) & 3) << 1) + (dy >> 1)
        spot = ((dy & 1) << 1) + rank
        for a in range(2):
            for c in range(2):
                placed[to, a, c, spot] = here[a, c, slot]
    for copy, onward in copies:
        copy.wait()
        onward.start()
    rows_out = pltpu.make_async_copy(placed, bsend, sems.at[5])
    rows_out.start()
    for copy, onward in copies:
        onward.wait()
    rows_out.wait()


def on_device(forward, backward_slab, slot_time, pattern, coupling, hamiltonian, lesser_now):
    smem = pl.BlockSpec(memory_space=pltpu.SMEM)
    vmem = pl.BlockSpec(memory_space=pltpu.VMEM)
    hbm = pl.BlockSpec(memory_space=pl.ANY)
    shape = jax.ShapeDtypeStruct
    bsend, f0, f1 = pl.pallas_call(
        pack,
        out_shape=(shape((8, 2, 2, 4, 16, N), bf), shape((2, 2, 2, N, N), bf), shape((2, 2, 2, N, N), bf)),
        in_specs=[smem, hbm, hbm],
        out_specs=(hbm, hbm, hbm),
        scratch_shapes=[pltpu.VMEM((2, 2, 32, 16, N), bf), pltpu.VMEM((8, 2, 2, 4, 16, N), bf),
                        pltpu.VMEM((4, 2, 2, N, N), bf), pltpu.SMEM((16,), jnp.int32),
                        pltpu.SemaphoreType.DMA((10,))],
        compiler_params=pltpu.CompilerParams(vmem_limit_bytes=61 << 20),
    )(slot_time, forward, backward_slab)
    moved = []
    for half, sent in enumerate((f0, f1)):
        pairs = []
        for e in range(16):
            for o in range(8):
                dy, dx = shift(o, half)
                d = ((e // 4 + dy) % 4) * 4 + (e % 4 + dx) % 4
                pairs.append((e * 8 + o, d * 8 + o))
        moved.append(lax.ppermute(sent, ("tm", "orb"), pairs))
    brecv = lax.all_to_all(bsend, "orb", 0, 0, tiled=True)
    V = pltpu.VMEM
    part = pl.pallas_call(
        collide,
        out_shape=shape((8, 2, 16, N), f32),
        in_specs=[smem] + [vmem] * 5,
        out_specs=vmem,
        scratch_shapes=[V((N, N, N), f32), V((N, N), f32), V((8, 2, N, N), f32), V((8, 2, N, N), f32),
                        V((8, N, 2 * N), f32), V((8, N, 2 * N), bf), pltpu.SMEM((4,), f32)],
        compiler_params=pltpu.CompilerParams(vmem_limit_bytes=24 << 20),
    )(slot_time, moved[0], moved[1], brecv, coupling, pattern)
    own = lax.all_to_all(part, "orb", 0, 0, tiled=True).sum(0)
    copies = jnp.broadcast_to(own.astype(bf)[None], (16,) + own.shape)
    spread = lax.all_to_all(copies, "tm", 0, 0, tiled=True).astype(f32)
    start = lax.axis_index("orb") * 16
    high = lax.Precision.HIGHEST
    ham_rows = lax.dynamic_slice_in_dim(hamiltonian, start, 16, 0)
    rows = lax.dynamic_slice_in_dim(lesser_now, start, 16, 1)
    ahead = jnp.dot(ham_rows, jnp.concatenate([lesser_now[0], lesser_now[1]], axis=1), precision=high)
    behind = jnp.dot(rows.reshape(32, N), hamiltonian, precision=high)
    comm_re = ahead[:, :N] - behind[:16]
    comm_im = ahead[:, N:] - behind[16:]
    base = rows + UPDATE_STEP * jnp.stack([comm_im, -comm_re])
    return base + spread.sum(0)


def solution(mesh):
    in_specs = (
        P(None, None, "tm", None, None),
        P(None, None, "tm", "orb", None),
        P(),
        P(),
        P(),
        P(),
        P(),
    )
    return jax.shard_map(on_device, mesh=mesh, in_specs=in_specs, out_specs=P(None, "orb", None), check_vma=False)
```

profile of v0, /device:TPU:1, one launch (start us, length us, event | category | flops | bytes accessed | tf_op | source)
XLA Modules:
  0.0 70.2 jit_solution(10698037499130616324)
XLA Ops:
  0.0 0.0 copy-start
  0.0 0.0 copy-start.1
  0.0 0.0 copy-start.2
  0.0 3.2 %shard_map.73 = (bf16[8,2,2,4,16,128]{5,4,3,2,1,0:T(8,128)(2,1)}, bf16[2,2,2,128,128]{4,3,2,1,0:T(8,128)(2,1)}, bf16[2,2,2,128,128]{4,3,2,1,0:T(8,128)(2,1)}) custom-call(s32[512]{0:T(512)} %times.3, bf16[2,2,32,128,128]{4,3,2,1,0:T(8,128)(2,1)} %fwd.1, bf16[2,2,32,16,128]{4,3,2,1,0:T(8,128)(2,1)} %slab.1), custom_call_target="tpu_custom_call" | custom-call | tf_op jit(solution)/shard_map/pallas_call | solution.py:246
  3.2 6.8 %all-to-all-start = ((bf16[8,2,2,4,16,128]{5,4,3,2,1,0:T(8,128)(2,1)}), bf16[8,2,2,4,16,128]{5,4,3,2,1,0:T(8,128)(2,1)S(1)}, u32[]{:S(2)}, u32[]{:S(2)}) async-start(bf16[8,2,2,4,16,128]{5,4,3,2,1,0:T(8,128)(2,1)} %get-tuple-element.10), calls=%async_computation | async-start | bytes 1048576 | tf_op jit(solution)/shard_map/all_to_all | solution.py:265
  10.0 7.3 %collective-permute-start = (bf16[2,2,2,128,128]{4,3,2,1,0:T(8,128)(2,1)}, bf16[2,2,2,128,128]{4,3,2,1,0:T(8,128)(2,1)S(1)}, u32[]{:S(2)}, u32[]{:S(2)}) collective-permute-start(bf16[2,2,2,128,128]{4,3,2,1,0:T(8,128)(2,1)} %get-tuple-element.8), channel_id=1, source_target_pairs={{0,0},{1,81},{2,10},{3,91},{4,20},{5,69},{6,30},{7,79},{8,8},{9,89... | collective-permute-start | bytes 786440 | tf_op jit(solution)/shard_map/ppermute | solution.py:264
  17.3 1.4 %collective-permute-start.1 = (bf16[2,2,2,128,128]{4,3,2,1,0:T(8,128)(2,1)}, bf16[2,2,2,128,128]{4,3,2,1,0:T(8,128)(2,1)S(1)}, u32[]{:S(2)}, u32[]{:S(2)}) collective-permute-start(bf16[2,2,2,128,128]{4,3,2,1,0:T(8,128)(2,1)} %get-tuple-element.9), channel_id=1, source_target_pairs={{0,40},{1,121},{2,50},{3,99},{4,60},{5,109},{6,38},{7,119},{8,48},... | collective-permute-start | bytes 786440 | tf_op jit(solution)/shard_map/ppermute | solution.py:264
  18.7 0.0 copy-done.4
  18.7 4.9 %collective-permute-done.f0 = bf16[2,2,2,128,128]{4,3,2,1,0:T(8,128)(2,1)S(1)} collective-permute-done((bf16[2,2,2,128,128]{4,3,2,1,0:T(8,128)(2,1)}, bf16[2,2,2,128,128]{4,3,2,1,0:T(8,128)(2,1)S(1)}, u32[]{:S(2)}, u32[]{:S(2)}) %collective-permute-start) | collective-permute-done | bytes 262176 | tf_op jit(solution)/shard_map/ppermute | solution.py:264
  23.6 2.1 %collective-permute-done.1.f1 = bf16[2,2,2,128,128]{4,3,2,1,0:T(8,128)(2,1)S(1)} collective-permute-done((bf16[2,2,2,128,128]{4,3,2,1,0:T(8,128)(2,1)}, bf16[2,2,2,128,128]{4,3,2,1,0:T(8,128)(2,1)S(1)}, u32[]{:S(2)}, u32[]{:S(2)}) %collective-permute-start.1) | collective-permute-done | bytes 262176 | tf_op jit(solution)/shard_map/ppermute | solution.py:264
  25.8 0.0 all-to-all-done.brecv
  25.8 0.0 copy-done.3
  25.8 0.0 copy-done.1
  25.8 0.0 copy-done.2
  25.8 22.7 %shard_map.74 = f32[8,2,16,128]{3,2,1,0:T(8,128)} custom-call(s32[512]{0:T(512)S(1)} %copy-done.3, bf16[2,2,2,128,128]{4,3,2,1,0:T(8,128)(2,1)S(1)} %collective-permute-done.f0, bf16[2,2,2,128,128]{4,3,2,1,0:T(8,128)(2,1)S(1)} %collective-permute-done.1.f1, bf16[8,2,2,4,16,128]{5,4,3,2,1,0:T(8,128)(2,1)S(1)} %all-to-all-done.brecv, ...), custom_call_target="tpu_custom_call" | custom-call | tf_op jit(solution)/shard_map/pallas_call | solution.py:267
  48.5 4.4 %all-to-all-start.1 = ((f32[8,2,16,128]{3,2,1,0:T(8,128)}), f32[8,2,16,128]{3,2,1,0:T(8,128)S(1)}, u32[]{:S(2)}, u32[]{:S(2)}) async-start(f32[8,2,16,128]{3,2,1,0:T(8,128)} %shard_map.74), calls=%async_computation.1 | async-start | bytes 262144 | tf_op jit(solution)/shard_map/all_to_all | solution.py:276
  52.9 0.0 copy-done
  52.9 0.2 fusion.12
  53.1 0.2 fusion
  53.3 4.9 %all-to-all-done.1 = f32[8,2,16,128]{3,2,1,0:T(8,128)S(1)} async-done(((f32[8,2,16,128]{3,2,1,0:T(8,128)}), f32[8,2,16,128]{3,2,1,0:T(8,128)S(1)}, u32[]{:S(2)}, u32[]{:S(2)}) %all-to-all-start.1) | async-done | bytes 131104 | tf_op jit(solution)/shard_map/all_to_all | solution.py:276
  58.2 0.7 broadcast_in_dim.2
  58.8 3.9 %all-to-all-start.2 = ((bf16[16,2,16,128]{3,2,1,0:T(8,128)(2,1)}), bf16[16,2,16,128]{3,2,1,0:T(8,128)(2,1)S(1)}, u32[]{:S(2)}, u32[]{:S(2)}) async-start(bf16[16,2,16,128]{3,2,1,0:T(8,128)(2,1)} %broadcast_in_dim.2), calls=%async_computation.2 | async-start | bytes 262144 | tf_op jit(solution)/shard_map/all_to_all | solution.py:278
  62.8 6.8 %all-to-all-done.2 = bf16[16,2,16,128]{3,2,1,0:T(8,128)(2,1)S(1)} async-done(((bf16[16,2,16,128]{3,2,1,0:T(8,128)(2,1)}), bf16[16,2,16,128]{3,2,1,0:T(8,128)(2,1)S(1)}, u32[]{:S(2)}, u32[]{:S(2)}) %all-to-all-start.2) | async-done | bytes 131104 | tf_op jit(solution)/shard_map/all_to_all | solution.py:278
  69.6 0.6 fusion.5
  (7 shorter events, 0.1 us)
Async XLA Ops:
  0.0 52.9 %copy-start = (f32[128,128]{1,0:T(8,128)S(1)}, f32[128,128]{1,0:T(8,128)}, u32[]{:S(2)}) copy-start(f32[128,128]{1,0:T(8,128)} %param.12) | copy-start | bytes 196612
  0.0 25.8 %copy-start.3 = (s32[512]{0:T(512)S(1)}, s32[512]{0:T(512)}, u32[]{:S(2)}) copy-start(s32[512]{0:T(512)} %times.3) | copy-start | bytes 6148
  0.0 18.7 %copy-start.4 = (f32[2,128,128]{2,1,0:T(8,128)S(1)}, f32[2,128,128]{2,1,0:T(8,128)}, u32[]{:S(2)}) copy-start(f32[2,128,128]{2,1,0:T(8,128)} %param.13) | copy-start | bytes 393220
  0.0 25.8 %copy-start.1 = (f32[128,128]{1,0:T(8,128)S(1)}, f32[128,128]{1,0:T(8,128)}, u32[]{:S(2)}) copy-start(f32[128,128]{1,0:T(8,128)} %coup.1) | copy-start | bytes 196612
  0.0 25.8 %copy-start.2 = (s32[128,128]{1,0:T(8,128)S(1)}, s32[128,128]{1,0:T(8,128)}, u32[]{:S(2)}) copy-start(s32[128,128]{1,0:T(8,128)} %patt.1) | copy-start | bytes 196612
  3.2 22.6 %all-to-all-start = ((bf16[8,2,2,4,16,128]{5,4,3,2,1,0:T(8,128)(2,1)}), bf16[8,2,2,4,16,128]{5,4,3,2,1,0:T(8,128)(2,1)S(1)}, u32[]{:S(2)}, u32[]{:S(2)}) async-start(bf16[8,2,2,4,16,128]{5,4,3,2,1,0:T(8,128)(2,1)} %get-tuple-element.10), calls=%async_computation | async-start | bytes 1048576 | tf_op jit(solution)/shard_map/all_to_all | solution.py:265
  10.0 13.6 %collective-permute-start = (bf16[2,2,2,128,128]{4,3,2,1,0:T(8,128)(2,1)}, bf16[2,2,2,128,128]{4,3,2,1,0:T(8,128)(2,1)S(1)}, u32[]{:S(2)}, u32[]{:S(2)}) collective-permute-start(bf16[2,2,2,128,128]{4,3,2,1,0:T(8,128)(2,1)} %get-tuple-element.8), channel_id=1, source_target_pairs={{0,0},{1,81},{2,10},{3,91},{4,20},{5,69},{6,30},{7,79},{8,8},{9,89... | collective-permute-start | bytes 786440 | tf_op jit(solution)/shard_map/ppermute | solution.py:264
  17.3 8.5 %collective-permute-start.1 = (bf16[2,2,2,128,128]{4,3,2,1,0:T(8,128)(2,1)}, bf16[2,2,2,128,128]{4,3,2,1,0:T(8,128)(2,1)S(1)}, u32[]{:S(2)}, u32[]{:S(2)}) collective-permute-start(bf16[2,2,2,128,128]{4,3,2,1,0:T(8,128)(2,1)} %get-tuple-element.9), channel_id=1, source_target_pairs={{0,40},{1,121},{2,50},{3,99},{4,60},{5,109},{6,38},{7,119},{8,48},... | collective-permute-start | bytes 786440 | tf_op jit(solution)/shard_map/ppermute | solution.py:264
  48.5 9.7 %all-to-all-start.1 = ((f32[8,2,16,128]{3,2,1,0:T(8,128)}), f32[8,2,16,128]{3,2,1,0:T(8,128)S(1)}, u32[]{:S(2)}, u32[]{:S(2)}) async-start(f32[8,2,16,128]{3,2,1,0:T(8,128)} %shard_map.74), calls=%async_computation.1 | async-start | bytes 262144 | tf_op jit(solution)/shard_map/all_to_all | solution.py:276
  58.8 10.8 %all-to-all-start.2 = ((bf16[16,2,16,128]{3,2,1,0:T(8,128)(2,1)}), bf16[16,2,16,128]{3,2,1,0:T(8,128)(2,1)S(1)}, u32[]{:S(2)}, u32[]{:S(2)}) async-start(bf16[16,2,16,128]{3,2,1,0:T(8,128)(2,1)} %broadcast_in_dim.2), calls=%async_computation.2 | async-start | bytes 262144 | tf_op jit(solution)/shard_map/all_to_all | solution.py:278
where the time goes:
time: 71.6 us; the launch traced here: 70.2 us
  Pallas kernels  25.9 us (36%)
  starting transfers between devices  23.8 us (33%)
  waiting for transfers between devices  18.8 us (26%)
    pallas_call x1, Pallas kernels, on_device(): pl.pallas_call(collide, out_shape=shape((8, 2, 16, N), f32), in_specs=[sm...  22.7 us
    ppermute x2, starting transfers between devices, on_device(): moved.append(lax.ppermute(sent, ('tm', 'orb'), pairs))  8.69 us
    ppermute x2, waiting for transfers between devices, on_device(): moved.append(lax.ppermute(sent, ('tm', 'orb'), pairs))  7.03 us
    all_to_all x1, waiting for transfers between devices, on_device(): spread = lax.all_to_all(copies, 'tm', 0, 0, tiled=True).astype(f32)  6.83 us
    all_to_all x1, starting transfers between devices, on_device(): brecv = lax.all_to_all(bsend, 'orb', 0, 0, tiled=True)  6.81 us
    all_to_all x1, waiting for transfers between devices, on_device(): own = lax.all_to_all(part, 'orb', 0, 0, tiled=True).sum(0)  4.9 us
    all_to_all x1, starting transfers between devices, on_device(): own = lax.all_to_all(part, 'orb', 0, 0, tiled=True).sum(0)  4.41 us
    all_to_all x1, starting transfers between devices, on_device(): spread = lax.all_to_all(copies, 'tm', 0, 0, tiled=True).astype(f32)  3.9 us
  transfers between devices with their start and end apart: 5, of which 4 were waited for; matrix products, arithmetic and copies ran while one was open for 0% of the time, Pallas kernels for 0%

commit v1 on v0

--- a/solution.py
+++ b/solution.py
@@ -191,8 +191,8 @@
         back_re = -0.5 * (re + re.T)
         back_im = 0.5 * (im - im.T)
         for o in range(8):
-            out[o, 0] = back_im[16 * o:16 * o + 16]
-            out[o, 1] = back_re[16 * o:16 * o + 16]
+            out[o, 0] = back_im[16 * o:16 * o + 16].astype(bf)
+            out[o, 1] = back_re[16 * o:16 * o + 16].astype(bf)
 
     pl.run_scoped(product, *[pltpu.ACC(kk % 2)((N, 2 * N), f32) for kk in range(4)])
 
@@ -266,14 +266,14 @@
     V = pltpu.VMEM
     part = pl.pallas_call(
         collide,
-        out_shape=shape((8, 2, 16, N), f32),
+        out_shape=shape((8, 2, 16, N), bf),
         in_specs=[smem] + [vmem] * 5,
         out_specs=vmem,
         scratch_shapes=[V((N, N, N), f32), V((N, N), f32), V((8, 2, N, N), f32), V((8, 2, N, N), f32),
                         V((8, N, 2 * N), f32), V((8, N, 2 * N), bf), pltpu.SMEM((4,), f32)],
         compiler_params=pltpu.CompilerParams(vmem_limit_bytes=24 << 20),
     )(slot_time, moved[0], moved[1], brecv, coupling, pattern)
-    own = lax.all_to_all(part, "orb", 0, 0, tiled=True).sum(0)
+    own = lax.all_to_all(part, "orb", 0, 0, tiled=True).astype(f32).sum(0)
     copies = jnp.broadcast_to(own.astype(bf)[None], (16,) + own.shape)
     spread = lax.all_to_all(copies, "tm", 0, 0, tiled=True).astype(f32)
     start = lax.axis_index("orb") * 16

time: 71.6 us -> 72.5 us (1.013)
  waiting for transfers between devices: 18.8 us -> 20.7 us
  starting transfers between devices: 23.8 us -> 23 us
    all_to_all x1, waiting for transfers between devices: 0.01 us -> 8.12 us  [on_device(): brecv = lax.all_to_all(bsend, 'orb', 0, 0, tiled=True)]
    ppermute x2, waiting for transfers between devices: 7.03 us -> 1.02 us  [on_device(): moved.append(lax.ppermute(sent, ('tm', 'orb'), pairs))]
    all_to_all x1, starting transfers between devices: 6.81 us -> 5.48 us  [on_device(): brecv = lax.all_to_all(bsend, 'orb', 0, 0, tiled=True)]
    ppermute x2, starting transfers between devices: 8.69 us -> 9.52 us  [on_device(): moved.append(lax.ppermute(sent, ('tm', 'orb'), pairs))]
where the time goes in v1:
time: 72.5 us; the launch traced here: 71.3 us
  Pallas kernels  25.9 us (36%)
  starting transfers between devices  23 us (32%)
  waiting for transfers between devices  20.7 us (29%)
    pallas_call x1, Pallas kernels, on_device(): pl.pallas_call(collide, out_shape=shape((8, 2, 16, N), bf), in_specs=[sme...  22.7 us
    ppermute x2, starting transfers between devices, on_device(): moved.append(lax.ppermute(sent, ('tm', 'orb'), pairs))  9.52 us
    all_to_all x1, waiting for transfers between devices, on_device(): brecv = lax.all_to_all(bsend, 'orb', 0, 0, tiled=True)  8.12 us
    all_to_all x1, waiting for transfers between devices, on_device(): spread = lax.all_to_all(copies, 'tm', 0, 0, tiled=True).astype(f32)  6.87 us
    all_to_all x1, starting transfers between devices, on_device(): brecv = lax.all_to_all(bsend, 'orb', 0, 0, tiled=True)  5.48 us
    all_to_all x1, waiting for transfers between devices, on_device(): own = lax.all_to_all(part, 'orb', 0, 0, tiled=True).astype(f32).sum(0)  4.71 us
    all_to_all x1, starting transfers between devices, on_device(): own = lax.all_to_all(part, 'orb', 0, 0, tiled=True).astype(f32).sum(0)  4.23 us
    all_to_all x1, starting transfers between devices, on_device(): spread = lax.all_to_all(copies, 'tm', 0, 0, tiled=True).astype(f32)  3.75 us
  transfers between devices with their start and end apart: 5, of which 4 were waited for; matrix products, arithmetic and copies ran while one was open for 0% of the time, Pallas kernels for 0%

profile of v1, /device:TPU:1, one launch (start us, length us, event | category | flops | bytes accessed | tf_op | source)
XLA Modules:
  0.0 71.3 jit_solution(11395431690510752421)
XLA Ops:
  0.0 0.0 copy-start
  0.0 0.0 copy-start.1
  0.0 0.0 copy-start.2
  0.0 3.2 %shard_map.73 = (bf16[8,2,2,4,16,128]{5,4,3,2,1,0:T(8,128)(2,1)}, bf16[2,2,2,128,128]{4,3,2,1,0:T(8,128)(2,1)}, bf16[2,2,2,128,128]{4,3,2,1,0:T(8,128)(2,1)}) custom-call(s32[512]{0:T(512)} %times.3, bf16[2,2,32,128,128]{4,3,2,1,0:T(8,128)(2,1)} %fwd.1, bf16[2,2,32,16,128]{4,3,2,1,0:T(8,128)(2,1)} %slab.1), custom_call_target="tpu_custom_call" | custom-call | tf_op jit(solution)/shard_map/pallas_call | solution.py:246
  3.2 8.1 %collective-permute-start = (bf16[2,2,2,128,128]{4,3,2,1,0:T(8,128)(2,1)}, bf16[2,2,2,128,128]{4,3,2,1,0:T(8,128)(2,1)S(1)}, u32[]{:S(2)}, u32[]{:S(2)}) collective-permute-start(bf16[2,2,2,128,128]{4,3,2,1,0:T(8,128)(2,1)} %get-tuple-element.8), channel_id=1, source_target_pairs={{0,0},{1,81},{2,10},{3,91},{4,20},{5,69},{6,30},{7,79},{8,8},{9,89... | collective-permute-start | bytes 786440 | tf_op jit(solution)/shard_map/ppermute | solution.py:264
  11.3 1.4 %collective-permute-start.1 = (bf16[2,2,2,128,128]{4,3,2,1,0:T(8,128)(2,1)}, bf16[2,2,2,128,128]{4,3,2,1,0:T(8,128)(2,1)S(1)}, u32[]{:S(2)}, u32[]{:S(2)}) collective-permute-start(bf16[2,2,2,128,128]{4,3,2,1,0:T(8,128)(2,1)} %get-tuple-element.9), channel_id=1, source_target_pairs={{0,40},{1,121},{2,50},{3,99},{4,60},{5,109},{6,38},{7,119},{8,48},... | collective-permute-start | bytes 786440 | tf_op jit(solution)/shard_map/ppermute | solution.py:264
  12.7 5.5 %all-to-all-start = ((bf16[8,2,2,4,16,128]{5,4,3,2,1,0:T(8,128)(2,1)}), bf16[8,2,2,4,16,128]{5,4,3,2,1,0:T(8,128)(2,1)S(1)}, u32[]{:S(2)}, u32[]{:S(2)}) async-start(bf16[8,2,2,4,16,128]{5,4,3,2,1,0:T(8,128)(2,1)} %get-tuple-element.10), calls=%async_computation | async-start | bytes 1048576 | tf_op jit(solution)/shard_map/all_to_all | solution.py:265
  18.2 0.0 copy-done.4
  18.2 0.0 copy-done
  18.2 0.2 fusion.12
  18.4 0.0 collective-permute-done.f0
  18.4 1.0 %collective-permute-done.1.f1 = bf16[2,2,2,128,128]{4,3,2,1,0:T(8,128)(2,1)S(1)} collective-permute-done((bf16[2,2,2,128,128]{4,3,2,1,0:T(8,128)(2,1)}, bf16[2,2,2,128,128]{4,3,2,1,0:T(8,128)(2,1)S(1)}, u32[]{:S(2)}, u32[]{:S(2)}) %collective-permute-start.1) | collective-permute-done | bytes 262176 | tf_op jit(solution)/shard_map/ppermute | solution.py:264
  19.4 8.1 %all-to-all-done.brecv = bf16[8,2,2,4,16,128]{5,4,3,2,1,0:T(8,128)(2,1)S(1)} async-done(((bf16[8,2,2,4,16,128]{5,4,3,2,1,0:T(8,128)(2,1)}), bf16[8,2,2,4,16,128]{5,4,3,2,1,0:T(8,128)(2,1)S(1)}, u32[]{:S(2)}, u32[]{:S(2)}) %all-to-all-start) | async-done | bytes 524320 | tf_op jit(solution)/shard_map/all_to_all | solution.py:265
  27.6 0.0 copy-done.3
  27.6 0.0 copy-done.1
  27.6 0.0 copy-done.2
  27.6 22.7 %shard_map.74 = bf16[8,2,16,128]{3,2,1,0:T(8,128)(2,1)} custom-call(s32[512]{0:T(512)S(1)} %copy-done.3, bf16[2,2,2,128,128]{4,3,2,1,0:T(8,128)(2,1)S(1)} %collective-permute-done.f0, bf16[2,2,2,128,128]{4,3,2,1,0:T(8,128)(2,1)S(1)} %collective-permute-done.1.f1, bf16[8,2,2,4,16,128]{5,4,3,2,1,0:T(8,128)(2,1)S(1)} %all-to-all-done.brecv, ...), custom_call_target="tpu_custom_call" | custom-call | tf_op jit(solution)/shard_map/pallas_call | solution.py:267
  50.3 4.2 %all-to-all-start.1 = ((bf16[8,2,16,128]{3,2,1,0:T(8,128)(2,1)}), bf16[8,2,16,128]{3,2,1,0:T(8,128)(2,1)S(1)}, u32[]{:S(2)}, u32[]{:S(2)}) async-start(bf16[8,2,16,128]{3,2,1,0:T(8,128)(2,1)} %shard_map.74), calls=%async_computation.1 | async-start | bytes 131072 | tf_op jit(solution)/shard_map/all_to_all | solution.py:276
  54.5 0.2 fusion
  54.7 4.7 %all-to-all-done.1 = bf16[8,2,16,128]{3,2,1,0:T(8,128)(2,1)S(1)} async-done(((bf16[8,2,16,128]{3,2,1,0:T(8,128)(2,1)}), bf16[8,2,16,128]{3,2,1,0:T(8,128)(2,1)S(1)}, u32[]{:S(2)}, u32[]{:S(2)}) %all-to-all-start.1) | async-done | bytes 65568 | tf_op jit(solution)/shard_map/all_to_all | solution.py:276
  59.4 0.7 broadcast_in_dim.2
  60.1 3.7 %all-to-all-start.2 = ((bf16[16,2,16,128]{3,2,1,0:T(8,128)(2,1)}), bf16[16,2,16,128]{3,2,1,0:T(8,128)(2,1)S(1)}, u32[]{:S(2)}, u32[]{:S(2)}) async-start(bf16[16,2,16,128]{3,2,1,0:T(8,128)(2,1)} %broadcast_in_dim.2), calls=%async_computation.2 | async-start | bytes 262144 | tf_op jit(solution)/shard_map/all_to_all | solution.py:278
  63.8 6.9 %all-to-all-done.2 = bf16[16,2,16,128]{3,2,1,0:T(8,128)(2,1)S(1)} async-done(((bf16[16,2,16,128]{3,2,1,0:T(8,128)(2,1)}), bf16[16,2,16,128]{3,2,1,0:T(8,128)(2,1)S(1)}, u32[]{:S(2)}, u32[]{:S(2)}) %all-to-all-start.2) | async-done | bytes 131104 | tf_op jit(solution)/shard_map/all_to_all | solution.py:278
  70.7 0.6 fusion.5
  (7 shorter events, 0.1 us)
Async XLA Ops:
  0.0 18.2 %copy-start = (f32[128,128]{1,0:T(8,128)S(1)}, f32[128,128]{1,0:T(8,128)}, u32[]{:S(2)}) copy-start(f32[128,128]{1,0:T(8,128)} %param.12) | copy-start | bytes 196612
  0.0 27.6 %copy-start.3 = (s32[512]{0:T(512)S(1)}, s32[512]{0:T(512)}, u32[]{:S(2)}) copy-start(s32[512]{0:T(512)} %times.3) | copy-start | bytes 6148
  0.0 18.2 %copy-start.4 = (f32[2,128,128]{2,1,0:T(8,128)S(1)}, f32[2,128,128]{2,1,0:T(8,128)}, u32[]{:S(2)}) copy-start(f32[2,128,128]{2,1,0:T(8,128)} %param.13) | copy-start | bytes 393220
  0.0 27.6 %copy-start.1 = (f32[128,128]{1,0:T(8,128)S(1)}, f32[128,128]{1,0:T(8,128)}, u32[]{:S(2)}) copy-start(f32[128,128]{1,0:T(8,128)} %coup.1) | copy-start | bytes 196612
  0.0 27.6 %copy-start.2 = (s32[128,128]{1,0:T(8,128)S(1)}, s32[128,128]{1,0:T(8,128)}, u32[]{:S(2)}) copy-start(s32[128,128]{1,0:T(8,128)} %patt.1) | copy-start | bytes 196612
  3.2 15.2 %collective-permute-start = (bf16[2,2,2,128,128]{4,3,2,1,0:T(8,128)(2,1)}, bf16[2,2,2,128,128]{4,3,2,1,0:T(8,128)(2,1)S(1)}, u32[]{:S(2)}, u32[]{:S(2)}) collective-permute-start(bf16[2,2,2,128,128]{4,3,2,1,0:T(8,128)(2,1)} %get-tuple-element.8), channel_id=1, source_target_pairs={{0,0},{1,81},{2,10},{3,91},{4,20},{5,69},{6,30},{7,79},{8,8},{9,89... | collective-permute-start | bytes 786440 | tf_op jit(solution)/shard_map/ppermute | solution.py:264
  11.3 8.1 %collective-permute-start.1 = (bf16[2,2,2,128,128]{4,3,2,1,0:T(8,128)(2,1)}, bf16[2,2,2,128,128]{4,3,2,1,0:T(8,128)(2,1)S(1)}, u32[]{:S(2)}, u32[]{:S(2)}) collective-permute-start(bf16[2,2,2,128,128]{4,3,2,1,0:T(8,128)(2,1)} %get-tuple-element.9), channel_id=1, source_target_pairs={{0,40},{1,121},{2,50},{3,99},{4,60},{5,109},{6,38},{7,119},{8,48},... | collective-permute-start | bytes 786440 | tf_op jit(solution)/shard_map/ppermute | solution.py:264
  12.7 14.8 %all-to-all-start = ((bf16[8,2,2,4,16,128]{5,4,3,2,1,0:T(8,128)(2,1)}), bf16[8,2,2,4,16,128]{5,4,3,2,1,0:T(8,128)(2,1)S(1)}, u32[]{:S(2)}, u32[]{:S(2)}) async-start(bf16[8,2,2,4,16,128]{5,4,3,2,1,0:T(8,128)(2,1)} %get-tuple-element.10), calls=%async_computation | async-start | bytes 1048576 | tf_op jit(solution)/shard_map/all_to_all | solution.py:265
  50.3 9.1 %all-to-all-start.1 = ((bf16[8,2,16,128]{3,2,1,0:T(8,128)(2,1)}), bf16[8,2,16,128]{3,2,1,0:T(8,128)(2,1)S(1)}, u32[]{:S(2)}, u32[]{:S(2)}) async-start(bf16[8,2,16,128]{3,2,1,0:T(8,128)(2,1)} %shard_map.74), calls=%async_computation.1 | async-start | bytes 131072 | tf_op jit(solution)/shard_map/all_to_all | solution.py:276
  60.1 10.6 %all-to-all-start.2 = ((bf16[16,2,16,128]{3,2,1,0:T(8,128)(2,1)}), bf16[16,2,16,128]{3,2,1,0:T(8,128)(2,1)S(1)}, u32[]{:S(2)}, u32[]{:S(2)}) async-start(bf16[16,2,16,128]{3,2,1,0:T(8,128)(2,1)} %broadcast_in_dim.2), calls=%async_computation.2 | async-start | bytes 262144 | tf_op jit(solution)/shard_map/all_to_all | solution.py:278
